TPU v7x, 128 devices: a whole 4x4x4 slice. The times are simulated.
128 devices in a mesh: bins: 16 (over y, z), chan: 8 (over x, core).
Axes of the slice: x: 4, y: 4, z: 4, core: 2. Of those that a mesh axis runs over, the one named last changes fastest.
Arguments:
- tokens_in: bfloat16 [8192, 2048], P('bins', 'chan'), may hold values from -6 to 6
- filters: bfloat16 [8192, 2048], P('bins', 'chan'), may hold values from -0.0625 to 0.0625
- gate: bfloat16 [8192, 2048], P('bins', 'chan'), may hold values from -6 to 6
- skip: float32 [2048], P('chan'), may hold values from 0.5 to 1.5
- out_grad: bfloat16 [8192, 4096], P('bins', 'chan'), may hold values from -6 to 6
- out_weight: bfloat16 [2048, 4096], P('chan'), may hold values from -0.09375 to 0.09375
- owner: int32 [16, 512], P(None, 'bins'), may hold values from 0 to 15, as said below
- slot: int32 [16, 512], P(None, 'bins'), may hold values from 0 to 1023, as said below
Outputs:
- gate_grad: bfloat16 [16, 512, 2048], P(None, 'bins', 'chan')
- filter_grad: float32 [16, 512, 2048], P(None, 'bins', 'chan')
- grad_rows: bfloat16 [16384, 2048], P('bins', 'chan')
Inputs may be any that keep to these rules, and one draw needn't show every extreme that they name: Let the column group j be the entries [i, r] with j * 32 <= r < (j + 1) * 32, all i. Within one column group at most 64 entries name the same owner, and in every draw some owner is named exactly 64 times by every column group. An entry of column group j (as for owner) lies in j * 64 to (j + 1) * 64 - 1; no two tokens share an owner and a slot; in every draw some owner has all 1024 slots used.
All inputs are finite; a program needn't handle non-finite values.
Results may differ from a plain program's by a relative error of at most 0.012.
Values may be sent and summed in bfloat16 or wider, within the bound.
A program may use at most 128 MiB of HBM per device.

v0:
```python
import math
import jax
import jax.numpy as jnp
from jax import lax
from jax.sharding import PartitionSpec as P

exact_mode = lax.Precision.HIGHEST


def angles(index, period):
    return 2.0 * math.pi / period * (index % period).astype(jnp.float32)


def contract(table, values, form):
    return jnp.einsum(form, table, values, precision=exact_mode)


def product(left_re, left_im, right_re, right_im):
    return (left_re * right_re - left_im * right_im, left_re * right_im + left_im * right_re)


def shards(tokens_in, filters, gate, skip, out_grad, out_weight, owner, slot):
    blocks = lax.axis_size("bins")
    my_index = lax.axis_index("bins")
    tok_rows, channels = tokens_in.shape
    col_rows = tok_rows // blocks
    length = 2 * blocks * tok_rows
    block_ids = jnp.arange(blocks, dtype=jnp.int32)
    bin_order = jnp.stack(
        [block_ids, jnp.where(block_ids == 0, blocks, 2 * blocks - block_ids)], axis=1
    ).reshape(2 * blocks)
    block_angle = angles(bin_order[:, None] * block_ids[None, :], 2 * blocks)
    block_cos = jnp.cos(block_angle)
    block_sin = jnp.sin(block_angle)
    back_cos = block_cos.T
    back_sin = block_sin.T
    column_ids = my_index * col_rows + jnp.arange(col_rows, dtype=jnp.int32)
    ahead_angle = angles(bin_order[:, None] * column_ids[None, :], length)[:, :, None]
    ahead_cos = jnp.cos(ahead_angle)
    ahead_sin = jnp.sin(ahead_angle)
    own_bins = lax.dynamic_slice_in_dim(bin_order, 2 * my_index, 2)
    positions = jnp.arange(tok_rows, dtype=jnp.int32)
    return_angle = angles(own_bins[:, None] * positions[None, :], length)[:, :, None]
    return_cos = jnp.cos(return_angle)
    return_sin = jnp.sin(return_angle)
    inner_angle = angles(positions[:, None] * positions[None, :], tok_rows)
    inner_cos = jnp.cos(inner_angle)
    inner_sin = jnp.sin(inner_angle)
    upstream = lax.dot_general(
        lax.all_gather(out_grad, "chan", axis=1, tiled=True),
        out_weight,
        (((1,), (1,)), ((), ())),
        preferred_element_type=jnp.float32,
    )
    g_rounded = upstream.astype(jnp.bfloat16)
    grad_in = (g_rounded.astype(jnp.float32) * gate.astype(jnp.float32)).astype(jnp.bfloat16)
    grid_shape = (blocks, col_rows, channels)
    tok_cols, filt_cols, grad_cols, gout_cols = (
        lax.all_to_all(
            tokens_in.reshape(grid_shape), "bins", split_axis=0, concat_axis=0, tiled=True
        ),
        lax.all_to_all(
            filters.reshape(grid_shape), "bins", split_axis=0, concat_axis=0, tiled=True
        ),
        lax.all_to_all(
            grad_in.reshape(grid_shape), "bins", split_axis=0, concat_axis=0, tiled=True
        ),
        lax.all_to_all(
            g_rounded.reshape(grid_shape), "bins", split_axis=0, concat_axis=0, tiled=True
        ),
    )
    tok_real = tok_cols.astype(jnp.float32)
    filt_real = filt_cols.astype(jnp.float32)
    grad_real = grad_cols.astype(jnp.float32)
    real_stack = jnp.stack([tok_real, filt_real, grad_real])
    part_re = contract(block_cos, real_stack, "ki,sirc->skrc")
    part_im = -contract(block_sin, real_stack, "ki,sirc->skrc")
    turned = jnp.stack(
        [part_re * ahead_cos + part_im * ahead_sin, part_im * ahead_cos - part_re * ahead_sin],
        axis=1,
    )
    arrived = lax.all_to_all(turned, "bins", split_axis=2, concat_axis=3, tiled=True)
    came_re = arrived[:, 0]
    came_im = arrived[:, 1]
    spec_re = contract(inner_cos, came_re, "kr,slrc->slkc") + contract(
        inner_sin, came_im, "kr,slrc->slkc"
    )
    spec_im = contract(inner_cos, came_im, "kr,slrc->slkc") - contract(
        inner_sin, came_re, "kr,slrc->slkc"
    )
    spec_re, spec_im = (spec_re, spec_im)
    x_re, x_im = (spec_re[0], spec_im[0])
    h_re, h_im = (spec_re[1], spec_im[1])
    y_re, y_im = (spec_re[2], spec_im[2])
    conv_re, conv_im = product(x_re, x_im, h_re, h_im)
    back_re, back_im = product(h_re, -h_im, y_re, y_im)
    lag_re, lag_im = product(y_re, y_im, x_re, -x_im)
    freq_re = jnp.stack([conv_re, back_re, lag_re])
    freq_im = jnp.stack([conv_im, back_im, lag_im])
    sum_re = contract(inner_cos, freq_re, "rk,slkc->slrc") - contract(
        inner_sin, freq_im, "rk,slkc->slrc"
    )
    sum_im = contract(inner_cos, freq_im, "rk,slkc->slrc") + contract(
        inner_sin, freq_re, "rk,slkc->slrc"
    )
    twist_re = sum_re * return_cos - sum_im * return_sin
    twist_im = sum_re * return_sin + sum_im * return_cos
    turned = jnp.stack([twist_re, twist_im], axis=1)
    arrived = lax.all_to_all(turned, "bins", split_axis=3, concat_axis=2, tiled=True)
    came_re = arrived[:, 0]
    came_im = arrived[:, 1]
    out_re = contract(back_cos, came_re, "ik,skrc->sirc") - contract(
        back_sin, came_im, "ik,skrc->sirc"
    )
    result_re = out_re / length
    conv = result_re[0]
    backward = result_re[1]
    lagged = result_re[2]
    gate_grad = (gout_cols.astype(jnp.float32) * (conv + skip * tok_real)).astype(jnp.bfloat16)
    filter_grad = lagged / math.sqrt(blocks * tok_rows)
    token_grad = (backward + skip * grad_real).astype(jnp.bfloat16)
    send_rows = 2 * tok_rows // blocks
    targets = owner.reshape(-1) * send_rows + slot.reshape(-1) - my_index * send_rows
    outbox = (
        jnp.zeros((blocks * send_rows, channels), jnp.bfloat16)
        .at[targets]
        .set(token_grad.reshape(tok_rows, channels))
    )
    inbox = lax.all_to_all(
        outbox.reshape(blocks, send_rows, channels), "bins", split_axis=0, concat_axis=0, tiled=True
    )
    grad_rows = inbox.reshape(blocks * send_rows, channels)
    return (gate_grad, filter_grad, grad_rows)


def solution(mesh):
    return jax.shard_map(
        shards,
        mesh=mesh,
        in_specs=(
            P("bins", "chan"),
            P("bins", "chan"),
            P("bins", "chan"),
            P("chan"),
            P("bins", "chan"),
            P("chan", None),
            P(None, "bins"),
            P(None, "bins"),
        ),
        out_specs=(P(None, "bins", "chan"), P(None, "bins", "chan"), P("bins", "chan")),
        check_vma=False,
    )
```

profile of v0, /device:TPU:0, one launch (start us, length us, event | category | flops | bytes accessed | tf_op | source)
XLA Modules:
  0.0 452.5 jit_solution(11163061509946371895)
XLA Ops:
  7.9 8.2 %all-to-all-start.1 = ((bf16[16,32,256]{2,1,0:T(8,128)(2,1)}), bf16[16,32,256]{2,1,0:T(8,128)(2,1)S(1)}, u32[]{:S(2)}, u32[]{:S(2)}) async-start(bf16[16,32,256]{2,1,0:T(8,128)(2,1)} %bitcast.142), calls=%async_computation.1 | async-start | bytes 524288 | tf_op jit(solution)/shard_map/all_to_all | solution.py:59
  16.5 8.1 %all-to-all-done.1 = bf16[16,32,256]{2,1,0:T(8,128)(2,1)S(1)} async-done(((bf16[16,32,256]{2,1,0:T(8,128)(2,1)}), bf16[16,32,256]{2,1,0:T(8,128)(2,1)S(1)}, u32[]{:S(2)}, u32[]{:S(2)}) %all-to-all-start.1) | async-done | bytes 262176 | tf_op jit(solution)/shard_map/all_to_all | solution.py:59
  24.6 3.6 all-to-all-start.2
  28.2 16.0 %all-gather.2.cloned.1.call-done = bf16[512,4096]{1,0:T(8,128)(2,1)} async-done(((bf16[512,512]{1,0:T(8,128)(2,1)}), bf16[512,4096]{1,0:T(8,128)(2,1)}) %all-gather.2.cloned.1.call-update) | async-done | bytes 4194320 | tf_op jit(solution)/shard_map/all_gather | solution.py:50
  44.2 4.3 multiply_convert_fusion
  48.5 7.2 %all-to-all-start.3 = ((bf16[16,32,256]{2,1,0:T(8,128)(2,1)}), bf16[16,32,256]{2,1,0:T(8,128)(2,1)S(1)}, u32[]{:S(2)}, u32[]{:S(2)}) async-start(bf16[16,32,256]{2,1,0:T(8,128)(2,1)} %bitcast.5), calls=%async_computation.3 | async-start | bytes 524288 | tf_op jit(solution)/shard_map/all_to_all | solution.py:65
  56.0 8.6 %all-to-all-done.3 = bf16[16,32,256]{2,1,0:T(8,128)(2,1)S(1)} async-done(((bf16[16,32,256]{2,1,0:T(8,128)(2,1)}), bf16[16,32,256]{2,1,0:T(8,128)(2,1)S(1)}, u32[]{:S(2)}, u32[]{:S(2)}) %all-to-all-start.3) | async-done | bytes 262176 | tf_op jit(solution)/shard_map/all_to_all | solution.py:65
  67.5 3.6 fusion.3
  72.3 6.3 %copy.48 = f32[3,2,32,32,256]{4,3,0,1,2:T(8,128)} copy(f32[3,2,32,32,256]{4,2,3,0,1:T(8,128)S(1)} %pad_maximum_fusion) | data formatting | bytes 12582912 | tf_op jit(solution)/shard_map/stack | solution.py:78
  78.5 4.9 %all-to-all-start.4 = ((f32[3,2,32,32,256]{4,3,0,1,2:T(8,128)}), f32[3,2,32,32,256]{4,3,0,1,2:T(8,128)}, u32[]{:S(2)}, u32[]{:S(2)}) async-start(f32[3,2,32,32,256]{4,3,0,1,2:T(8,128)} %copy.48), calls=%async_computation.4 | async-start | bytes 12582912 | tf_op jit(solution)/shard_map/all_to_all | solution.py:82
  83.6 97.4 %all-to-all-done.4 = f32[3,2,32,32,256]{4,3,0,1,2:T(8,128)} async-done(((f32[3,2,32,32,256]{4,3,0,1,2:T(8,128)}), f32[3,2,32,32,256]{4,3,0,1,2:T(8,128)}, u32[]{:S(2)}, u32[]{:S(2)}) %all-to-all-start.4) | async-done | bytes 6291488 | tf_op jit(solution)/shard_map/all_to_all | solution.py:82
  181.1 3.5 copy.50
  184.6 14.7 %fusion.7 = f32[3,2,256,512]{3,2,1,0:T(8,128)S(1)} fusion(f32[3,2,2,512,256]{4,3,2,1,0:T(8,128)S(1)} %bitcast.136), kind=kOutput, calls=%fused_computation.24 | convolution fusion | flops 4835508224 | bytes 6291456 | tf_op jit(solution)/shard_map/kr,slrc->slkc/dot_general | solution.py:15
  199.3 14.5 %fusion.6 = f32[3,2,256,512]{3,2,1,0:T(8,128)S(1)} fusion(f32[3,2,2,512,256]{4,3,2,1,0:T(8,128)S(1)} %bitcast.137), kind=kOutput, calls=%fused_computation.23 | convolution fusion | flops 4835508224 | bytes 6291456 | tf_op jit(solution)/shard_map/kr,slrc->slkc/dot_general | solution.py:15
  213.8 14.6 %add_bitcast_fusion.1 = f32[3,2,512,256]{2,3,1,0:T(8,128)S(1)} fusion(f32[3,2,256,512]{3,2,1,0:T(8,128)S(1)} %fusion.7, f32[3,2,2,512,256]{4,3,2,1,0:T(8,128)S(1)} %bitcast.138), kind=kOutput, calls=%fused_computation.22 | convolution fusion | flops 4836294656 | bytes 9437184 | tf_op jit(solution)/shard_map/kr,slrc->slkc/dot_general | solution.py:15
  228.4 14.5 %subtract_bitcast_fusion.1 = f32[3,2,512,256]{2,3,1,0:T(8,128)S(1)} fusion(f32[3,2,256,512]{3,2,1,0:T(8,128)S(1)} %fusion.6, f32[3,2,2,512,256]{4,3,2,1,0:T(8,128)S(1)} %bitcast.139), kind=kOutput, calls=%fused_computation.21 | convolution fusion | flops 4836294656 | bytes 9437184 | tf_op jit(solution)/shard_map/kr,slrc->slkc/dot_general | solution.py:15
  244.5 9.5 %fusion.10 = f32[3,2,256,512]{3,2,1,0:T(8,128)S(1)} fusion(f32[1,2,512,256]{2,3,1,0:T(8,128)S(1)} %get-tuple-element.22, f32[1,2,512,256]{2,3,1,0:T(8,128)S(1)} %get-tuple-element.21, f32[1,2,512,256]{2,3,1,0:T(8,128)S(1)} %get-tuple-element.24), kind=kOutput, calls=%fused_computation.27 | convolution fusion | flops 4837081088 | bytes 6291456 | tf_op jit(solution)/shard_map/rk,slkc->slrc/dot_general | solution.py:15
  254.0 9.4 %fusion.11 = f32[3,2,256,512]{3,2,1,0:T(8,128)S(1)} fusion(f32[1,2,512,256]{2,3,1,0:T(8,128)S(1)} %get-tuple-element.22, f32[1,2,512,256]{2,3,1,0:T(8,128)S(1)} %get-tuple-element.21, f32[1,2,512,256]{2,3,1,0:T(8,128)S(1)} %get-tuple-element.24), kind=kOutput, calls=%fused_computation.28 | convolution fusion | flops 4837081088 | bytes 6291456 | tf_op jit(solution)/shard_map/rk,slkc->slrc/dot_general | solution.py:15
  263.4 9.8 %fusion.14 = f32[3,2,256,512]{3,2,1,0:T(8,128)S(1)} fusion(f32[3,2,256,512]{3,2,1,0:T(8,128)S(1)} %fusion.11, f32[1,2,512,256]{2,3,1,0:T(8,128)S(1)} %get-tuple-element.20, f32[1,2,512,256]{2,3,1,0:T(8,128)S(1)} %get-tuple-element.23, f32[1,2,512,256]{2,3,1,0:T(8,128)S(1)} %get-tuple-element.19), kind=kOutput, calls=%fused_computation.31 | convolution fusion | flops 4837867520 | bytes 9437184 | tf_op jit(solution)/shard_map/rk,slkc->slrc/dot_general | solution.py:15
  273.2 9.9 %subtract_bitcast_fusion = (f32[3,1,2,512,256]{3,4,2,0,1:T(8,128)S(1)}, f32[3,1,2,512,256]{3,4,2,0,1:T(8,128)S(1)}) fusion(f32[3,2,256,512]{3,2,1,0:T(8,128)S(1)} %fusion.14, f32[2,512]{1,0:T(2,128)S(1)} %get-tuple-element.30, f32[2,512]{1,0:T(2,128)S(1)} %get-tuple-element.29, f32[3,2,256,512]{3,2,1,0:T(8,128)S(1)} %fusion.10, ...), kind=kOutput, calls=%fused_computation.20 | convolution fusion | flops 4842586112 | bytes 15736832 | tf_op jit(solution)/shard_map/rk,slkc->slrc/dot_general | solution.py:15
  283.1 3.5 pad_maximum_fusion.1
  286.7 10.5 %copy.53 = f32[3,2,2,512,256]{4,2,0,1,3:T(2,128)} copy(f32[3,2,2,512,256]{3,4,2,0,1:T(8,128)} %pad_maximum_fusion.1) | data formatting | bytes 12582912 | tf_op jit(solution)/shard_map/stack | solution.py:108
  297.1 9.0 %all-to-all-start.5 = ((f32[3,2,2,512,256]{4,2,0,1,3:T(2,128)}), f32[3,2,2,512,256]{4,2,0,1,3:T(2,128)}, u32[]{:S(2)}, u32[]{:S(2)}) async-start(f32[3,2,2,512,256]{4,2,0,1,3:T(2,128)} %copy.53), calls=%async_computation.5 | async-start | bytes 12582912 | tf_op jit(solution)/shard_map/all_to_all | solution.py:109
  306.3 77.4 %all-to-all-done.5 = f32[3,2,2,512,256]{4,2,0,1,3:T(2,128)} async-done(((f32[3,2,2,512,256]{4,2,0,1,3:T(2,128)}), f32[3,2,2,512,256]{4,2,0,1,3:T(2,128)}, u32[]{:S(2)}, u32[]{:S(2)}) %all-to-all-start.5) | async-done | bytes 6291488 | tf_op jit(solution)/shard_map/all_to_all | solution.py:109
  383.7 4.3 all-to-all-start
  388.0 6.6 %copy.54 = f32[3,2,2,512,256]{4,3,2,1,0:T(8,128)} copy(f32[3,2,2,512,256]{4,2,0,1,3:T(2,128)} %all-to-all-done.5) | data formatting | bytes 12582912 | tf_op jit(solution)/shard_map/all_to_all | solution.py:109
  394.6 10.3 %copy.55 = f32[3,2,16,2,32,256]{5,3,2,4,0,1:T(2,128)} copy(f32[3,2,16,2,32,256]{5,4,2,3,1,0:T(8,128)} %bitcast.140) | data formatting | bytes 12582912 | tf_op jit(solution)/shard_map/all_to_all | solution.py:109
  404.9 8.5 %all_to_all.52 = f32[3,2,32,32,256]{4,2,3,0,1:T(8,128)} reshape(f32[3,2,16,2,32,256]{5,3,2,4,0,1:T(2,128)} %copy.55) | data formatting | bytes 12582912 | tf_op jit(solution)/shard_map/all_to_all | solution.py:109
  413.4 3.7 fusion
  417.1 4.9 %multiply_bitcast_fusion = f32[3,16,32,256]{3,1,2,0:T(8,128)} fusion(f32[3,32,256,16]{2,3,1,0:T(8,128)S(1)} %fusion, f32[3,2,32,32,256]{4,2,3,0,1:T(8,128)} %all_to_all.52, s32[32]{0:T(128)S(1)} %mul.319), kind=kOutput, calls=%fused_computation.34 | convolution fusion | flops 151788544 | bytes 6291584 | tf_op jit(solution)/shard_map/ik,skrc->sirc/dot_general | solution.py:15
  427.3 7.2 %all-to-all-start.6 = ((bf16[16,64,256]{2,1,0:T(8,128)(2,1)}), bf16[16,64,256]{2,1,0:T(8,128)(2,1)S(1)}, u32[]{:S(2)}, u32[]{:S(2)}) async-start(bf16[16,64,256]{2,1,0:T(8,128)(2,1)} %bitcast.44), calls=%async_computation.6 | async-start | bytes 1048576 | tf_op jit(solution)/shard_map/all_to_all | solution.py:129
  437.5 7.1 %all-to-all-done.6 = bf16[16,64,256]{2,1,0:T(8,128)(2,1)S(1)} async-done(((bf16[16,64,256]{2,1,0:T(8,128)(2,1)}), bf16[16,64,256]{2,1,0:T(8,128)(2,1)S(1)}, u32[]{:S(2)}, u32[]{:S(2)}) %all-to-all-start.6) | async-done | bytes 524320 | tf_op jit(solution)/shard_map/all_to_all | solution.py:129
  (40 shorter events, 16.4 us)
Async XLA Ops:
  7.2 37.1 %copy-start = (bf16[256,4096]{1,0:T(8,128)(2,1)S(1)}, bf16[256,4096]{1,0:T(8,128)(2,1)}, u32[]{:S(2)}) copy-start(bf16[256,4096]{1,0:T(8,128)(2,1)} %param.13) | copy-start | bytes 6291460
  7.2 37.0 %all-gather.2.cloned.1.call-start = ((), (), s32[]{:S(2)}) async-start(), calls=%async_computation.7 | async-start | bytes 4718592 | tf_op jit(solution)/shard_map/all_gather | solution.py:50
  7.9 16.7 %all-to-all-start.1 = ((bf16[16,32,256]{2,1,0:T(8,128)(2,1)}), bf16[16,32,256]{2,1,0:T(8,128)(2,1)S(1)}, u32[]{:S(2)}, u32[]{:S(2)}) async-start(bf16[16,32,256]{2,1,0:T(8,128)(2,1)} %bitcast.142), calls=%async_computation.1 | async-start | bytes 524288 | tf_op jit(solution)/shard_map/all_to_all | solution.py:59
  24.6 23.9 %all-to-all-start.2 = ((bf16[16,32,256]{2,1,0:T(8,128)(2,1)}), bf16[16,32,256]{2,1,0:T(8,128)(2,1)S(1)}, u32[]{:S(2)}, u32[]{:S(2)}) async-start(bf16[16,32,256]{2,1,0:T(8,128)(2,1)} %bitcast.143), calls=%async_computation.2 | async-start | bytes 524288 | tf_op jit(solution)/shard_map/all_to_all | solution.py:62
  48.5 16.1 %all-to-all-start.3 = ((bf16[16,32,256]{2,1,0:T(8,128)(2,1)}), bf16[16,32,256]{2,1,0:T(8,128)(2,1)S(1)}, u32[]{:S(2)}, u32[]{:S(2)}) async-start(bf16[16,32,256]{2,1,0:T(8,128)(2,1)} %bitcast.5), calls=%async_computation.3 | async-start | bytes 524288 | tf_op jit(solution)/shard_map/all_to_all | solution.py:65
  78.5 102.5 %all-to-all-start.4 = ((f32[3,2,32,32,256]{4,3,0,1,2:T(8,128)}), f32[3,2,32,32,256]{4,3,0,1,2:T(8,128)}, u32[]{:S(2)}, u32[]{:S(2)}) async-start(f32[3,2,32,32,256]{4,3,0,1,2:T(8,128)} %copy.48), calls=%async_computation.4 | async-start | bytes 12582912 | tf_op jit(solution)/shard_map/all_to_all | solution.py:82
  297.1 9.0 %copy-start.2 = (s32[16,32]{1,0:T(8,128)S(1)}, s32[16,32]{1,0:T(8,128)}, u32[]{:S(2)}) copy-start(s32[16,32]{1,0:T(8,128)} %param.15) | copy-start | bytes 6148
  297.1 9.1 %copy-start.3 = (s32[16,32]{1,0:T(8,128)S(1)}, s32[16,32]{1,0:T(8,128)}, u32[]{:S(2)}) copy-start(s32[16,32]{1,0:T(8,128)} %param.14) | copy-start | bytes 6148
  297.1 86.5 %all-to-all-start.5 = ((f32[3,2,2,512,256]{4,2,0,1,3:T(2,128)}), f32[3,2,2,512,256]{4,2,0,1,3:T(2,128)}, u32[]{:S(2)}, u32[]{:S(2)}) async-start(f32[3,2,2,512,256]{4,2,0,1,3:T(2,128)} %copy.53), calls=%async_computation.5 | async-start | bytes 12582912 | tf_op jit(solution)/shard_map/all_to_all | solution.py:109
  383.7 38.3 %all-to-all-start = ((bf16[16,32,256]{2,1,0:T(8,128)(2,1)}), bf16[16,32,256]{2,1,0:T(8,128)(2,1)S(1)}, u32[]{:S(2)}, u32[]{:S(2)}) async-start(bf16[16,32,256]{2,1,0:T(8,128)(2,1)} %bitcast), calls=%async_computation | async-start | bytes 524288 | tf_op jit(solution)/shard_map/all_to_all | solution.py:68
  417.1 4.9 %copy-start.4 = (f32[256]{0:T(256)S(1)}, f32[256]{0:T(256)}, u32[]{:S(2)}) copy-start(f32[256]{0:T(256)} %param.11) | copy-start | bytes 3076
  422.0 23.4 %copy-start.1 = (bf16[256,4096]{1,0:T(8,128)(2,1)S(1)}, bf16[256,4096]{1,0:T(8,128)(2,1)}, u32[]{:S(2)}) copy-start(bf16[256,4096]{1,0:T(8,128)(2,1)} %param.13) | copy-start | bytes 6291460
  427.3 17.3 %all-to-all-start.6 = ((bf16[16,64,256]{2,1,0:T(8,128)(2,1)}), bf16[16,64,256]{2,1,0:T(8,128)(2,1)S(1)}, u32[]{:S(2)}, u32[]{:S(2)}) async-start(bf16[16,64,256]{2,1,0:T(8,128)(2,1)} %bitcast.44), calls=%async_computation.6 | async-start | bytes 1048576 | tf_op jit(solution)/shard_map/all_to_all | solution.py:129
Sparse Core Ops, SparseCore 0:
  9.7 34.4 all-gather.1
where the time goes:
time: 456 us; the launch traced here: 452 us
  waiting for transfers between devices  215 us (47%)
  matrix products  116 us (25%)
  local copies, waits for them, and re-layouts  52.1 us (11%)
  starting transfers between devices  44.4 us (10%)
  between operations  14.5 us (3%)
  other arithmetic  9.98 us (2%)
    dot_general x12, matrix products, contract(): return jnp.einsum(form, table, values, precision=exact_mode)  112 us
    all_to_all x1, waiting for transfers between devices, shards(): lax.all_to_all(turned, 'bins', split_axis=2, concat_axis=3, tiled=True)  97.4 us
    all_to_all x1, waiting for transfers between devices, shards(): lax.all_to_all(turned, 'bins', split_axis=3, concat_axis=2, tiled=True)  77.4 us
    all_to_all x3, local copies, waits for them, and re-layouts, shards(): lax.all_to_all(turned, 'bins', split_axis=3, concat_axis=2, tiled=True)  25.4 us
    all_gather x1, waiting for transfers between devices, shards(): lax.all_gather(out_grad, 'chan', axis=1, tiled=True)  16 us
    another operation x1, local copies, waits for them, and re-layouts, shards(): turned = jnp.stack([twist_re, twist_im], axis=1)  10.5 us
  transfers between devices with their start and end apart: 8, of which 6 were waited for; matrix products, arithmetic and copies ran while one was open for 7% of the time, Pallas kernels for 0%

commit v1 on v0

--- a/solution.py
+++ b/solution.py
@@ -5,6 +5,13 @@
 from jax.sharding import PartitionSpec as P
 
 exact_mode = lax.Precision.HIGHEST
+
+
+def exchange_gather(shard, mesh_axis, along):
+    devices = lax.axis_size(mesh_axis)
+    blocks = jnp.stack([shard for _ in range(devices)])
+    blocks = lax.all_to_all(blocks, mesh_axis, split_axis=0, concat_axis=0)
+    return jnp.concatenate(blocks, axis=along)
 
 
 def angles(index, period):
@@ -47,7 +54,7 @@
     inner_cos = jnp.cos(inner_angle)
     inner_sin = jnp.sin(inner_angle)
     upstream = lax.dot_general(
-        lax.all_gather(out_grad, "chan", axis=1, tiled=True),
+        exchange_gather(out_grad, "chan", 1),
         out_weight,
         (((1,), (1,)), ((), ())),
         preferred_element_type=jnp.float32,

time: 456 us -> 463 us (1.015)
  between operations: 14.5 us -> 1.18 us
  waiting for transfers between devices: 215 us -> 228 us
    all_to_all x0 -> x1, waiting for transfers between devices: none -> 49.3 us  [exchange_gather(): blocks = lax.all_to_all(blocks, mesh_axis, split_axis=0, concat_axis=0)]
    all_to_all x1, waiting for transfers between devices: 97.4 us -> 77.7 us  [shards(): lax.all_to_all(turned, 'bins', split_axis=2, concat_axis=3, tiled=True)]
    all_gather x1 -> x0, waiting for transfers between devices: 16 us -> none  [shards(): lax.all_gather(out_grad, 'chan', axis=1, tiled=True)]
    all_to_all x0 -> x1, starting transfers between devices: none -> 4.7 us  [exchange_gather(): blocks = lax.all_to_all(blocks, mesh_axis, split_axis=0, concat_axis=0)]
  transfers between devices with their start and end apart: 8 -> 8, of which waited for: 6 -> 7; matrix products, arithmetic and copies ran while one was open for 7% -> 8% of each run, Pallas kernels for 0% -> 0%
where the time goes in v1:
time: 463 us; the launch traced here: 458 us
  waiting for transfers between devices  228 us (49%)
  matrix products  116 us (25%)
  local copies, waits for them, and re-layouts  55.8 us (12%)
  starting transfers between devices  47.3 us (10%)
  other arithmetic  9.97 us (2%)
    dot_general x12, matrix products, contract(): return jnp.einsum(form, table, values, precision=exact_mode)  112 us
    all_to_all x1, waiting for transfers between devices, shards(): lax.all_to_all(turned, 'bins', split_axis=2, concat_axis=3, tiled=True)  77.7 us
    all_to_all x1, waiting for transfers between devices, shards(): lax.all_to_all(turned, 'bins', split_axis=3, concat_axis=2, tiled=True)  73.9 us
    all_to_all x1, waiting for transfers between devices, exchange_gather(): blocks = lax.all_to_all(blocks, mesh_axis, split_axis=0, concat_axis=0)  49.3 us
    all_to_all x3, local copies, waits for them, and re-layouts, shards(): lax.all_to_all(turned, 'bins', split_axis=3, concat_axis=2, tiled=True)  25.4 us
    another operation x1, local copies, waits for them, and re-layouts, shards(): turned = jnp.stack([twist_re, twist_im], axis=1)  10.5 us
  transfers between devices with their start and end apart: 8, of which 7 were waited for; matrix products, arithmetic and copies ran while one was open for 8% of the time, Pallas kernels for 0%

profile of v1, /device:TPU:0, one launch (start us, length us, event | category | flops | bytes accessed | tf_op | source)
XLA Modules:
  0.0 458.0 jit_solution(4435090065130905610)
XLA Ops:
  0.6 8.3 %all-to-all-start.2 = ((bf16[16,32,256]{2,1,0:T(8,128)(2,1)}), bf16[16,32,256]{2,1,0:T(8,128)(2,1)S(1)}, u32[]{:S(2)}, u32[]{:S(2)}) async-start(bf16[16,32,256]{2,1,0:T(8,128)(2,1)} %bitcast.145), calls=%async_computation.2 | async-start | bytes 524288 | tf_op jit(solution)/shard_map/all_to_all | solution.py:66
  10.2 7.3 %all-to-all-done.2 = bf16[16,32,256]{2,1,0:T(8,128)(2,1)S(1)} async-done(((bf16[16,32,256]{2,1,0:T(8,128)(2,1)}), bf16[16,32,256]{2,1,0:T(8,128)(2,1)S(1)}, u32[]{:S(2)}, u32[]{:S(2)}) %all-to-all-start.2) | async-done | bytes 262176 | tf_op jit(solution)/shard_map/all_to_all | solution.py:66
  19.9 4.7 %all-to-all-start = ((bf16[8,512,512]{1,2,0:T(8,128)(2,1)}), bf16[8,512,512]{1,2,0:T(8,128)(2,1)}, u32[]{:S(2)}, u32[]{:S(2)}) async-start(bf16[8,512,512]{1,2,0:T(8,128)(2,1)} %stack.61), calls=%async_computation | async-start | bytes 8388608 | tf_op jit(solution)/shard_map/all_to_all | solution.py:13
  25.0 49.3 %all-to-all-done = bf16[8,512,512]{1,2,0:T(8,128)(2,1)} async-done(((bf16[8,512,512]{1,2,0:T(8,128)(2,1)}), bf16[8,512,512]{1,2,0:T(8,128)(2,1)}, u32[]{:S(2)}, u32[]{:S(2)}) %all-to-all-start) | async-done | bytes 4194336 | tf_op jit(solution)/shard_map/all_to_all | solution.py:13
  74.2 3.6 all-to-all-start.3
  77.9 4.3 multiply_convert_fusion
  82.1 4.2 all-to-all-done.3
  86.4 3.8 all-to-all-start.4
  90.5 8.1 %all-to-all-done.4 = bf16[16,32,256]{2,1,0:T(8,128)(2,1)S(1)} async-done(((bf16[16,32,256]{2,1,0:T(8,128)(2,1)}), bf16[16,32,256]{2,1,0:T(8,128)(2,1)S(1)}, u32[]{:S(2)}, u32[]{:S(2)}) %all-to-all-start.4) | async-done | bytes 262176 | tf_op jit(solution)/shard_map/all_to_all | solution.py:72
  101.6 3.6 fusion.3
  106.3 6.3 %copy.51 = f32[3,2,32,32,256]{4,3,0,1,2:T(8,128)} copy(f32[3,2,32,32,256]{4,2,3,0,1:T(8,128)S(1)} %pad_maximum_fusion) | data formatting | bytes 12582912 | tf_op jit(solution)/shard_map/stack | solution.py:85
  112.6 4.9 %all-to-all-start.5 = ((f32[3,2,32,32,256]{4,3,0,1,2:T(8,128)}), f32[3,2,32,32,256]{4,3,0,1,2:T(8,128)}, u32[]{:S(2)}, u32[]{:S(2)}) async-start(f32[3,2,32,32,256]{4,3,0,1,2:T(8,128)} %copy.51), calls=%async_computation.5 | async-start | bytes 12582912 | tf_op jit(solution)/shard_map/all_to_all | solution.py:89
  117.7 77.7 %all-to-all-done.5 = f32[3,2,32,32,256]{4,3,0,1,2:T(8,128)} async-done(((f32[3,2,32,32,256]{4,3,0,1,2:T(8,128)}), f32[3,2,32,32,256]{4,3,0,1,2:T(8,128)}, u32[]{:S(2)}, u32[]{:S(2)}) %all-to-all-start.5) | async-done | bytes 6291488 | tf_op jit(solution)/shard_map/all_to_all | solution.py:89
  198.9 14.7 %fusion.7 = f32[3,2,256,512]{3,2,1,0:T(8,128)S(1)} fusion(f32[3,2,2,512,256]{4,3,2,1,0:T(8,128)S(1)} %bitcast.139), kind=kOutput, calls=%fused_computation.24 | convolution fusion | flops 4835508224 | bytes 6291456 | tf_op jit(solution)/shard_map/kr,slrc->slkc/dot_general | solution.py:22
  213.6 14.5 %fusion.6 = f32[3,2,256,512]{3,2,1,0:T(8,128)S(1)} fusion(f32[3,2,2,512,256]{4,3,2,1,0:T(8,128)S(1)} %bitcast.140), kind=kOutput, calls=%fused_computation.23 | convolution fusion | flops 4835508224 | bytes 6291456 | tf_op jit(solution)/shard_map/kr,slrc->slkc/dot_general | solution.py:22
  228.2 14.6 %add_bitcast_fusion.1 = f32[3,2,512,256]{2,3,1,0:T(8,128)S(1)} fusion(f32[3,2,256,512]{3,2,1,0:T(8,128)S(1)} %fusion.7, f32[3,2,2,512,256]{4,3,2,1,0:T(8,128)S(1)} %bitcast.141), kind=kOutput, calls=%fused_computation.22 | convolution fusion | flops 4836294656 | bytes 9437184 | tf_op jit(solution)/shard_map/kr,slrc->slkc/dot_general | solution.py:22
  242.8 14.5 %subtract_bitcast_fusion.1 = f32[3,2,512,256]{2,3,1,0:T(8,128)S(1)} fusion(f32[3,2,256,512]{3,2,1,0:T(8,128)S(1)} %fusion.6, f32[3,2,2,512,256]{4,3,2,1,0:T(8,128)S(1)} %bitcast.142), kind=kOutput, calls=%fused_computation.21 | convolution fusion | flops 4836294656 | bytes 9437184 | tf_op jit(solution)/shard_map/kr,slrc->slkc/dot_general | solution.py:22
  258.9 9.5 %fusion.10 = f32[3,2,256,512]{3,2,1,0:T(8,128)S(1)} fusion(f32[1,2,512,256]{2,3,1,0:T(8,128)S(1)} %get-tuple-element.22, f32[1,2,512,256]{2,3,1,0:T(8,128)S(1)} %get-tuple-element.21, f32[1,2,512,256]{2,3,1,0:T(8,128)S(1)} %get-tuple-element.24), kind=kOutput, calls=%fused_computation.27 | convolution fusion | flops 4837081088 | bytes 6291456 | tf_op jit(solution)/shard_map/rk,slkc->slrc/dot_general | solution.py:22
  268.3 9.4 %fusion.11 = f32[3,2,256,512]{3,2,1,0:T(8,128)S(1)} fusion(f32[1,2,512,256]{2,3,1,0:T(8,128)S(1)} %get-tuple-element.22, f32[1,2,512,256]{2,3,1,0:T(8,128)S(1)} %get-tuple-element.21, f32[1,2,512,256]{2,3,1,0:T(8,128)S(1)} %get-tuple-element.24), kind=kOutput, calls=%fused_computation.28 | convolution fusion | flops 4837081088 | bytes 6291456 | tf_op jit(solution)/shard_map/rk,slkc->slrc/dot_general | solution.py:22
  277.8 9.8 %fusion.14 = f32[3,2,256,512]{3,2,1,0:T(8,128)S(1)} fusion(f32[3,2,256,512]{3,2,1,0:T(8,128)S(1)} %fusion.11, f32[1,2,512,256]{2,3,1,0:T(8,128)S(1)} %get-tuple-element.20, f32[1,2,512,256]{2,3,1,0:T(8,128)S(1)} %get-tuple-element.23, f32[1,2,512,256]{2,3,1,0:T(8,128)S(1)} %get-tuple-element.19), kind=kOutput, calls=%fused_computation.31 | convolution fusion | flops 4837867520 | bytes 9437184 | tf_op jit(solution)/shard_map/rk,slkc->slrc/dot_general | solution.py:22
  287.6 9.9 %subtract_bitcast_fusion = (f32[3,1,2,512,256]{3,4,2,0,1:T(8,128)S(1)}, f32[3,1,2,512,256]{3,4,2,0,1:T(8,128)S(1)}) fusion(f32[3,2,256,512]{3,2,1,0:T(8,128)S(1)} %fusion.14, f32[2,512]{1,0:T(2,128)S(1)} %get-tuple-element.30, f32[2,512]{1,0:T(2,128)S(1)} %get-tuple-element.29, f32[3,2,256,512]{3,2,1,0:T(8,128)S(1)} %fusion.10, ...), kind=kOutput, calls=%fused_computation.20 | convolution fusion | flops 4842586112 | bytes 15736832 | tf_op jit(solution)/shard_map/rk,slkc->slrc/dot_general | solution.py:22
  301.0 10.5 %copy.56 = f32[3,2,2,512,256]{4,2,0,1,3:T(2,128)} copy(f32[3,2,2,512,256]{3,4,2,0,1:T(8,128)} %pad_maximum_fusion.1) | data formatting | bytes 12582912 | tf_op jit(solution)/shard_map/stack | solution.py:115
  311.5 8.4 %all-to-all-start.6 = ((f32[3,2,2,512,256]{4,2,0,1,3:T(2,128)}), f32[3,2,2,512,256]{4,2,0,1,3:T(2,128)}, u32[]{:S(2)}, u32[]{:S(2)}) async-start(f32[3,2,2,512,256]{4,2,0,1,3:T(2,128)} %copy.56), calls=%async_computation.6 | async-start | bytes 12582912 | tf_op jit(solution)/shard_map/all_to_all | solution.py:116
  320.0 73.9 %all-to-all-done.6 = f32[3,2,2,512,256]{4,2,0,1,3:T(2,128)} async-done(((f32[3,2,2,512,256]{4,2,0,1,3:T(2,128)}), f32[3,2,2,512,256]{4,2,0,1,3:T(2,128)}, u32[]{:S(2)}, u32[]{:S(2)}) %all-to-all-start.6) | async-done | bytes 6291488 | tf_op jit(solution)/shard_map/all_to_all | solution.py:116
  393.9 6.4 %all-to-all-start.1 = ((bf16[16,32,256]{2,1,0:T(8,128)(2,1)}), bf16[16,32,256]{2,1,0:T(8,128)(2,1)S(1)}, u32[]{:S(2)}, u32[]{:S(2)}) async-start(bf16[16,32,256]{2,1,0:T(8,128)(2,1)} %bitcast.2), calls=%async_computation.1 | async-start | bytes 524288 | tf_op jit(solution)/shard_map/all_to_all | solution.py:75
  400.3 6.6 %copy.57 = f32[3,2,2,512,256]{4,3,2,1,0:T(8,128)} copy(f32[3,2,2,512,256]{4,2,0,1,3:T(2,128)} %all-to-all-done.6) | data formatting | bytes 12582912 | tf_op jit(solution)/shard_map/all_to_all | solution.py:116
  406.9 10.3 %copy.58 = f32[3,2,16,2,32,256]{5,3,2,4,0,1:T(2,128)} copy(f32[3,2,16,2,32,256]{5,4,2,3,1,0:T(8,128)} %bitcast.143) | data formatting | bytes 12582912 | tf_op jit(solution)/shard_map/all_to_all | solution.py:116
  417.2 8.5 %all_to_all.56 = f32[3,2,32,32,256]{4,2,3,0,1:T(8,128)} reshape(f32[3,2,16,2,32,256]{5,3,2,4,0,1:T(2,128)} %copy.58) | data formatting | bytes 12582912 | tf_op jit(solution)/shard_map/all_to_all | solution.py:116
  425.7 3.7 fusion
  429.4 4.9 %multiply_bitcast_fusion = f32[3,16,32,256]{3,1,2,0:T(8,128)} fusion(f32[3,32,256,16]{2,3,1,0:T(8,128)S(1)} %fusion, f32[3,2,32,32,256]{4,2,3,0,1:T(8,128)} %all_to_all.56, s32[32]{0:T(128)S(1)} %mul.319), kind=kOutput, calls=%fused_computation.34 | convolution fusion | flops 151788544 | bytes 6291584 | tf_op jit(solution)/shard_map/ik,skrc->sirc/dot_general | solution.py:22
  439.6 7.2 %all-to-all-start.7 = ((bf16[16,64,256]{2,1,0:T(8,128)(2,1)}), bf16[16,64,256]{2,1,0:T(8,128)(2,1)S(1)}, u32[]{:S(2)}, u32[]{:S(2)}) async-start(bf16[16,64,256]{2,1,0:T(8,128)(2,1)} %bitcast.46), calls=%async_computation.7 | async-start | bytes 1048576 | tf_op jit(solution)/shard_map/all_to_all | solution.py:136
  449.8 7.1 %all-to-all-done.7 = bf16[16,64,256]{2,1,0:T(8,128)(2,1)S(1)} async-done(((bf16[16,64,256]{2,1,0:T(8,128)(2,1)}), bf16[16,64,256]{2,1,0:T(8,128)(2,1)S(1)}, u32[]{:S(2)}, u32[]{:S(2)}) %all-to-all-start.7) | async-done | bytes 524320 | tf_op jit(solution)/shard_map/all_to_all | solution.py:136
  (43 shorter events, 26.4 us)
Async XLA Ops:
  0.6 77.2 %copy-start = (bf16[256,4096]{1,0:T(8,128)(2,1)S(1)}, bf16[256,4096]{1,0:T(8,128)(2,1)}, u32[]{:S(2)}) copy-start(bf16[256,4096]{1,0:T(8,128)(2,1)} %param.13) | copy-start | bytes 6291460
  0.6 16.8 %all-to-all-start.2 = ((bf16[16,32,256]{2,1,0:T(8,128)(2,1)}), bf16[16,32,256]{2,1,0:T(8,128)(2,1)S(1)}, u32[]{:S(2)}, u32[]{:S(2)}) async-start(bf16[16,32,256]{2,1,0:T(8,128)(2,1)} %bitcast.145), calls=%async_computation.2 | async-start | bytes 524288 | tf_op jit(solution)/shard_map/all_to_all | solution.py:66
  19.9 58.0 %copy-start.5 = (bf16[512,256]{1,0:T(8,128)(2,1)S(1)}, bf16[512,256]{1,0:T(8,128)(2,1)}, u32[]{:S(2)}) copy-start(bf16[512,256]{1,0:T(8,128)(2,1)} %param.10) | copy-start | bytes 786436
  19.9 54.3 %all-to-all-start = ((bf16[8,512,512]{1,2,0:T(8,128)(2,1)}), bf16[8,512,512]{1,2,0:T(8,128)(2,1)}, u32[]{:S(2)}, u32[]{:S(2)}) async-start(bf16[8,512,512]{1,2,0:T(8,128)(2,1)} %stack.61), calls=%async_computation | async-start | bytes 8388608 | tf_op jit(solution)/shard_map/all_to_all | solution.py:13
  74.2 12.1 %all-to-all-start.3 = ((bf16[16,32,256]{2,1,0:T(8,128)(2,1)}), bf16[16,32,256]{2,1,0:T(8,128)(2,1)S(1)}, u32[]{:S(2)}, u32[]{:S(2)}) async-start(bf16[16,32,256]{2,1,0:T(8,128)(2,1)} %bitcast.5), calls=%async_computation.3 | async-start | bytes 524288 | tf_op jit(solution)/shard_map/all_to_all | solution.py:69
  86.4 12.3 %all-to-all-start.4 = ((bf16[16,32,256]{2,1,0:T(8,128)(2,1)}), bf16[16,32,256]{2,1,0:T(8,128)(2,1)S(1)}, u32[]{:S(2)}, u32[]{:S(2)}) async-start(bf16[16,32,256]{2,1,0:T(8,128)(2,1)} %bitcast.7), calls=%async_computation.4 | async-start | bytes 524288 | tf_op jit(solution)/shard_map/all_to_all | solution.py:72
  112.6 82.8 %all-to-all-start.5 = ((f32[3,2,32,32,256]{4,3,0,1,2:T(8,128)}), f32[3,2,32,32,256]{4,3,0,1,2:T(8,128)}, u32[]{:S(2)}, u32[]{:S(2)}) async-start(f32[3,2,32,32,256]{4,3,0,1,2:T(8,128)} %copy.51), calls=%async_computation.5 | async-start | bytes 12582912 | tf_op jit(solution)/shard_map/all_to_all | solution.py:89
  311.5 8.4 %copy-start.2 = (s32[16,32]{1,0:T(8,128)S(1)}, s32[16,32]{1,0:T(8,128)}, u32[]{:S(2)}) copy-start(s32[16,32]{1,0:T(8,128)} %param.15) | copy-start | bytes 6148
  311.5 8.4 %copy-start.3 = (s32[16,32]{1,0:T(8,128)S(1)}, s32[16,32]{1,0:T(8,128)}, u32[]{:S(2)}) copy-start(s32[16,32]{1,0:T(8,128)} %param.14) | copy-start | bytes 6148
  311.5 82.4 %all-to-all-start.6 = ((f32[3,2,2,512,256]{4,2,0,1,3:T(2,128)}), f32[3,2,2,512,256]{4,2,0,1,3:T(2,128)}, u32[]{:S(2)}, u32[]{:S(2)}) async-start(f32[3,2,2,512,256]{4,2,0,1,3:T(2,128)} %copy.56), calls=%async_computation.6 | async-start | bytes 12582912 | tf_op jit(solution)/shard_map/all_to_all | solution.py:116
  393.9 40.4 %all-to-all-start.1 = ((bf16[16,32,256]{2,1,0:T(8,128)(2,1)}), bf16[16,32,256]{2,1,0:T(8,128)(2,1)S(1)}, u32[]{:S(2)}, u32[]{:S(2)}) async-start(bf16[16,32,256]{2,1,0:T(8,128)(2,1)} %bitcast.2), calls=%async_computation.1 | async-start | bytes 524288 | tf_op jit(solution)/shard_map/all_to_all | solution.py:75
  429.4 4.9 %copy-start.4 = (f32[256]{0:T(256)S(1)}, f32[256]{0:T(256)}, u32[]{:S(2)}) copy-start(f32[256]{0:T(256)} %param.11) | copy-start | bytes 3076
  434.3 23.4 %copy-start.1 = (bf16[256,4096]{1,0:T(8,128)(2,1)S(1)}, bf16[256,4096]{1,0:T(8,128)(2,1)}, u32[]{:S(2)}) copy-start(bf16[256,4096]{1,0:T(8,128)(2,1)} %param.13) | copy-start | bytes 6291460
  439.6 17.3 %all-to-all-start.7 = ((bf16[16,64,256]{2,1,0:T(8,128)(2,1)}), bf16[16,64,256]{2,1,0:T(8,128)(2,1)S(1)}, u32[]{:S(2)}, u32[]{:S(2)}) async-start(bf16[16,64,256]{2,1,0:T(8,128)(2,1)} %bitcast.46), calls=%async_computation.7 | async-start | bytes 1048576 | tf_op jit(solution)/shard_map/all_to_all | solution.py:136
